TPU v7x, 256 devices: a whole 4x4x8 slice. The times are simulated.
256 devices in a mesh: row: 8 (over z), col: 32 (over x, y, core).
Axes of the slice: x: 4, y: 4, z: 8, core: 2. Of those that a mesh axis runs over, the one named last changes fastest.
Arguments:
- h_values: float32 [8, 512, 4096], P('row', 'col'), as said below
- h_places: int32 [8, 512], P('row', 'col'), may hold values from 0 to 15, as said below
- h_counts: int32 [8, 32], P('row', 'col'), may hold values from 0 to 16, as said below
- p_values: float32 [8, 512, 4096], P('row', 'col'), as said below
- p_places: int32 [8, 512], P('row', 'col'), may hold values from 0 to 15, as said below
- p_counts: int32 [8, 32], P('row', 'col'), may hold values from 0 to 16, as said below
- s_values: float32 [8, 512, 4096], P('row', 'col'), as said below
- s_places: int32 [8, 512], P('row', 'col'), may hold values from 0 to 15, as said below
- s_counts: int32 [8, 32], P('row', 'col'), may hold values from 0 to 16, as said below
- x_places: int32 [8, 512], P('row', 'col'), may hold values from 0 to 15, as said below
- x_counts: int32 [8, 32], P('row', 'col'), may hold values from 0 to 16, as said below
Outputs:
- gradient: float32 [8, 512, 4096], P('row', 'col')
Inputs may be any that keep to these rules, and one draw needn't show every extreme that they name: `h_places`: in each tile the 16 entries are a permutation of the tile's positions; the first count entries are the present blocks. Every pattern is symmetric, holds every block whose block row and block column lie in the same row panel, and every block (i, j) whose cyclic block distance min(|i - j|, 64 - |i - j|) is 2 or less or exactly 32. `p_places`: as for h_places. `s_places`: as for h_places. `x_places`: as for h_places. `h_counts`: every tile whose block columns lie in its own row panel is full. `p_counts`: as for h_counts. `s_counts`: as for h_counts. `x_counts`: as for h_counts. `h_values`: the assembled H is symmetric. `p_values`: the assembled P is symmetric. `s_values`: the assembled S is symmetric.
All inputs are finite; a program needn't handle non-finite values.
Results may differ from a plain program's by a relative error of at most 0.000088.
Values sent between devices are 32-bit elements; how exact they have to be, the bound alone decides.
A program may use at most 64 MiB of HBM per device.

v0:
```python
import jax
import jax.numpy as jnp
from jax import lax
from jax.sharding import PartitionSpec as P

BS = 64
TC = 2


def from_root(value, axis, source):
    kept = jnp.where(lax.axis_index(axis) == source, value, 0).astype(value.dtype)
    return lax.psum(kept, axis)


def assemble(values, places, counts):
    blocks_in = values[0]
    capacity = blocks_in.shape[0]
    slot_ids = lax.iota(jnp.int32, capacity)
    matches = (places[0][:, None] == slot_ids[None, :]) & (slot_ids[:, None] < counts[0, 0])
    spread = jnp.dot(matches.astype(jnp.float32).T, blocks_in, precision=lax.Precision.HIGHEST)
    row_count = capacity // TC
    return (
        spread.reshape(row_count, TC, BS, BS).transpose(0, 2, 1, 3).reshape(row_count * BS, TC * BS)
    )


def expand_mask(present, row_count, col_count):
    flags = present.reshape(row_count, col_count)
    return jnp.broadcast_to(flags[:, None, :, None], (row_count, BS, col_count, BS)).reshape(
        row_count * BS, col_count * BS
    )


def tile_mask(places, counts):
    capacity = places.shape[1]
    slot_ids = lax.iota(jnp.int32, capacity)
    matches = (places[0][:, None] == slot_ids[None, :]) & (slot_ids[:, None] < counts[0, 0])
    present = jnp.sum(matches.astype(jnp.float32), axis=0)
    return expand_mask(present, capacity // TC, TC)


def tile_to_slots(tile, places, counts):
    row_count = tile.shape[0] // BS
    blocks = (
        tile.reshape(row_count, BS, TC, BS).transpose(0, 2, 1, 3).reshape(row_count * TC, BS * BS)
    )
    picked = jnp.take(blocks, places[0], axis=0)
    slot_ids = lax.iota(jnp.int32, places.shape[1])
    used = (slot_ids < counts[0, 0]).astype(jnp.float32)
    return (picked * used[:, None])[None]


def shards(
    h_values,
    h_places,
    h_counts,
    p_values,
    p_places,
    p_counts,
    s_values,
    s_places,
    s_counts,
    x_places,
    x_counts,
):
    col_index = lax.axis_index("col")
    h_tile = assemble(h_values, h_places, h_counts)
    p_tile = assemble(p_values, p_places, p_counts)
    s_tile = assemble(s_values, s_places, s_counts)
    mask_tile = tile_mask(x_places, x_counts)
    row_width = h_tile.shape[0]
    col_width = h_tile.shape[1]
    p_columns, s_columns = (
        lax.all_gather(p_tile, "row", axis=0, tiled=True),
        lax.all_gather(s_tile, "row", axis=0, tiled=True),
    )
    product = jnp.dot(
        lax.all_gather(h_tile, "col", axis=1, tiled=True),
        p_columns,
        precision=lax.Precision.HIGHEST,
    )
    y_tile = mask_tile * product
    y_panel = lax.all_gather(y_tile, "col", axis=1, tiled=True)
    x_tile = mask_tile * jnp.dot(y_panel, s_columns, precision=lax.Precision.HIGHEST)
    per_panel = row_width // col_width
    source_row = col_index // per_panel
    offset = col_index % per_panel * col_width
    y_part = lax.dynamic_slice_in_dim(y_panel, offset, col_width, 0)
    y_mirror = from_root(y_part, "row", source_row)
    far_part = lax.dot_general(
        lax.all_gather(s_tile, "col", axis=1, tiled=True),
        y_mirror,
        (((1,), (1,)), ((), ())),
        precision=lax.Precision.HIGHEST,
    )
    mirrored = mask_tile * far_part
    return tile_to_slots(x_tile + mirrored, x_places, x_counts)


def solution(mesh):
    in_specs = (
        P("row", "col", None),
        P("row", "col"),
        P("row", "col"),
        P("row", "col", None),
        P("row", "col"),
        P("row", "col"),
        P("row", "col", None),
        P("row", "col"),
        P("row", "col"),
        P("row", "col"),
        P("row", "col"),
    )
    out_specs = P("row", "col", None)
    return jax.shard_map(shards, mesh=mesh, in_specs=in_specs, out_specs=out_specs, check_vma=False)
```

profile of v0, /device:TPU:2, one launch (start us, length us, event | category | flops | bytes accessed | tf_op | source)
XLA Modules:
  0.0 405.1 jit_solution(8840308818379448259)
XLA Ops:
  7.3 1.1 dot_general.34
  8.4 1.3 convolution_bitcast_fusion.1
  9.8 0.3 copy.26
  10.0 0.9 reshape.190
  11.9 0.7 convolution_bitcast_fusion.2
  12.8 0.9 reshape.189
  14.8 0.3 reshape.188
  15.2 40.0 %all-gather.8.cloned.1.call-done = f32[4096,128]{0,1:T(8,128)} async-done(((f32[512,128]{0,1:T(8,128)}), f32[4096,128]{0,1:T(8,128)}) %all-gather.8.cloned.1.call-update) | async-done | bytes 2097168 | tf_op jit(solution)/shard_map/all_gather | solution.py:74
  55.1 59.1 %all-gather.6.cloned.1.call-done = f32[512,4096]{0,1:T(8,128)} async-done(((f32[512,128]{0,1:T(8,128)}), f32[512,4096]{0,1:T(8,128)}) %all-gather.6.cloned.1.call-update) | async-done | bytes 8388624 | tf_op jit(solution)/shard_map/all_gather | solution.py:78
  114.2 16.5 %convolution_multiply_fusion = f32[512,128]{1,0:T(8,128)} fusion(f32[512,128]{1,0:T(8,128)S(1)} %reshape.188, f32[512,4096]{0,1:T(8,128)} %all-gather.6.cloned.1.call-done, f32[4096,128]{0,1:T(8,128)} %all-gather.8.cloned.1.call-done), kind=kOutput, calls=%fused_computation.7 | convolution fusion | flops 3221291008 | bytes 11010048 | tf_op jit(solution)/shard_map/dot_general | solution.py:77
  131.7 0.7 convolution_bitcast_fusion
  132.4 0.3 copy.28
  132.7 0.9 reshape.191
  133.6 0.5 all-gather.14.cloned.1.call-update
  134.4 60.4 %all-gather.10.cloned.1.call-done = f32[512,4096]{1,0:T(8,128)} async-done(((f32[512,128]{1,0:T(8,128)}), f32[512,4096]{1,0:T(8,128)}) %all-gather.10.cloned.1.call-update) | async-done | bytes 8388624 | tf_op jit(solution)/shard_map/all_gather | solution.py:83
  194.8 3.2 dynamic-slice_select_fusion
  198.0 39.7 %all-gather.12.cloned.1.call-done = f32[4096,128]{0,1:T(8,128)} async-done(((f32[512,128]{0,1:T(8,128)}), f32[4096,128]{0,1:T(8,128)}) %all-gather.12.cloned.1.call-update) | async-done | bytes 2097168 | tf_op jit(solution)/shard_map/all_gather | solution.py:75
  237.7 9.3 %fusion.29 = f32[512,128]{1,0:T(8,128)S(1)} fusion(f32[512,4096]{1,0:T(8,128)} %all-gather.10.cloned.1.call-done, f32[4096,128]{0,1:T(8,128)} %all-gather.12.cloned.1.call-done), kind=kOutput, calls=%fused_computation.48 | convolution fusion | flops 3221225472 | bytes 10747904 | tf_op jit(solution)/shard_map/dot_general | solution.py:84
  247.0 49.5 %all-gather.14.cloned.1.call-done = f32[512,4096]{0,1:T(8,128)} async-done(((f32[512,128]{0,1:T(8,128)}), f32[512,4096]{0,1:T(8,128)}) %all-gather.14.cloned.1.call-update) | async-done | bytes 8388624 | tf_op jit(solution)/shard_map/all_gather | solution.py:91
  296.6 83.7 %all-reduce.2.cloned.1.call-done = f32[128,4096]{1,0:T(8,128)} async-done(((f32[128,4096]{1,0:T(8,128)}), f32[128,4096]{1,0:T(8,128)}) %all-reduce.2.cloned.1.call-update) | async-done | bytes 2097168 | tf_op jit(solution)/shard_map/psum | solution.py:12
  380.3 16.0 %fusion = f32[512,128]{1,0:T(8,128)S(1)} fusion(f32[512,128]{1,0:T(8,128)S(1)} %reshape.188, f32[512,128]{1,0:T(8,128)S(1)} %fusion.29, f32[512,4096]{0,1:T(8,128)} %all-gather.14.cloned.1.call-done, f32[128,4096]{1,0:T(8,128)} %all-reduce.2.cloned.1.call-done), kind=kOutput, calls=%fused_computation.6 | convolution fusion | flops 3221356544 | bytes 11272192 | tf_op jit(solution)/shard_map/dot_general | solution.py:90
  396.3 0.3 reshape.192
  396.9 0.6 gather_fusion
  397.5 0.8 fusion.7
  (37 shorter events, 1.8 us)
Async XLA Ops:
  6.5 5.1 %copy-start = (f32[1,16,4096]{2,1,0:T(8,128)S(1)}, f32[1,16,4096]{2,1,0:T(8,128)}, u32[]{:S(2)}) copy-start(f32[1,16,4096]{2,1,0:T(8,128)} %param.11) | copy-start | bytes 786436
  6.5 48.6 %all-gather.8.cloned.1.call-start = ((), (), s32[]{:S(2)}) async-start(), calls=%async_computation.1 | async-start | bytes 2359296 | tf_op jit(solution)/shard_map/all_gather | solution.py:74
  8.4 3.5 copy-start.2
  10.9 3.5 copy-start.4
  10.9 103.3 %all-gather.6.cloned.1.call-start = ((), (), s32[]{:S(2)}) async-start(), calls=%async_computation | async-start | bytes 8650752 | tf_op jit(solution)/shard_map/all_gather | solution.py:78
  13.7 181.1 %all-gather.10.cloned.1.call-start = ((), (), s32[]{:S(2)}) async-start(), calls=%async_computation.2 | async-start | bytes 8650752 | tf_op jit(solution)/shard_map/all_gather | solution.py:83
  15.1 116.3 %copy-start.1 = (f32[1,16,4096]{2,1,0:T(8,128)S(1)}, f32[1,16,4096]{2,1,0:T(8,128)}, u32[]{:S(2)}) copy-start(f32[1,16,4096]{2,1,0:T(8,128)} %param.17) | copy-start | bytes 786436
  15.2 116.5 %copy-start.3 = (s32[1,16]{1,0:T(1,128)S(1)}, s32[1,16]{1,0:T(1,128)}, u32[]{:S(2)}) copy-start(s32[1,16]{1,0:T(1,128)} %param.18) | copy-start | bytes 196
  130.8 106.9 %all-gather.12.cloned.1.call-start = ((), (), s32[]{:S(2)}) async-start(), calls=%async_computation.3 | async-start | bytes 2359296 | tf_op jit(solution)/shard_map/all_gather | solution.py:75
  133.6 163.0 %all-gather.14.cloned.1.call-start = ((), (), s32[]{:S(2)}) async-start(), calls=%async_computation.4 | async-start | bytes 8650752 | tf_op jit(solution)/shard_map/all_gather | solution.py:91
  134.2 246.2 %all-reduce.2.cloned.1.call-start = ((), (), s32[]{:S(2)}) async-start(), calls=%async_computation.5 | async-start | bytes 4194304 | tf_op jit(solution)/shard_map/psum | solution.py:12
Sparse Core Ops, SparseCore 0:
  11.1 44.0 all-gather.7
  57.7 56.4 all-gather.5
  130.9 63.8 all-gather.9
  196.5 41.1 all-gather.11
  240.1 56.4 all-gather.13
  298.8 81.4 all-reduce.1
where the time goes:
time: 405 us
  waiting for transfers between devices  333 us (82%)
  matrix products  44.6 us (11%)
  between operations  16.4 us (4%)
  local copies, waits for them, and re-layouts  6.76 us (2%)
  other arithmetic  4.09 us (1%)
    psum x1, waiting for transfers between devices, from_root(): return lax.psum(kept, axis)  83.7 us
    all_gather x1, waiting for transfers between devices, shards(): y_panel = lax.all_gather(y_tile, 'col', axis=1, tiled=True)  60.4 us
    all_gather x1, waiting for transfers between devices, shards(): lax.all_gather(h_tile, 'col', axis=1, tiled=True)  59.1 us
    all_gather x1, waiting for transfers between devices, shards(): lax.all_gather(s_tile, 'col', axis=1, tiled=True)  49.5 us
    all_gather x1, waiting for transfers between devices, shards(): lax.all_gather(p_tile, 'row', axis=0, tiled=True)  40 us
    all_gather x1, waiting for transfers between devices, shards(): lax.all_gather(s_tile, 'row', axis=0, tiled=True)  39.7 us
    dot_general x1, matrix products, shards(): jnp.dot(lax.all_gather(h_tile, 'col', axis=1, tiled=True), p_columns, pre...  16.5 us
    dot_general x1, matrix products, shards(): lax.dot_general(lax.all_gather(s_tile, 'col', axis=1, tiled=True), y_mirr...  16 us
  transfers between devices with their start and end apart: 6, of which 6 were waited for; matrix products, arithmetic and copies ran while one was open for 4% of the time, Pallas kernels for 0%

commit v1 on v0

--- a/solution.py
+++ b/solution.py
@@ -5,6 +5,28 @@
 
 BS = 64
 TC = 2
+
+
+def joined_along(parts, dim):
+    parts = jnp.moveaxis(parts, 0, dim)
+    lengths = parts.shape
+    return parts.reshape(*lengths[:dim], lengths[dim] * lengths[dim + 1], *lengths[dim + 2 :])
+
+
+def collect(value, axis, dim):
+    length = lax.axis_size(axis)
+    pairs = [(i, (i + 1) % length) for i in range(length)]
+    back = [(b, a) for a, b in pairs]
+    lower, upper = ([], [])
+    for step in range(length - 1):
+        if step % 2 == 0:
+            lower.append(lax.ppermute(lower[-1] if lower else value, axis, pairs))
+        else:
+            upper.append(lax.ppermute(upper[-1] if upper else value, axis, back))
+    tiles = jnp.stack([*lower[::-1], value, *upper])
+    shift = lax.axis_index(axis) - len(lower)
+    tiles = tiles[(jnp.arange(length) - shift) % length]
+    return joined_along(tiles, dim)
 
 
 def from_root(value, axis, source):
@@ -71,7 +93,7 @@
     row_width = h_tile.shape[0]
     col_width = h_tile.shape[1]
     p_columns, s_columns = (
-        lax.all_gather(p_tile, "row", axis=0, tiled=True),
+        collect(p_tile, "row", 0),
         lax.all_gather(s_tile, "row", axis=0, tiled=True),
     )
     product = jnp.dot(

time: 405 us -> 363 us (0.90)
  waiting for transfers between devices: 333 us -> 269 us
  starting transfers between devices: 0.39 us -> 12.4 us
  local copies, waits for them, and re-layouts: 6.76 us -> 16.3 us
    all_gather x1, waiting for transfers between devices: 59.1 us -> 12.5 us  [shards(): lax.all_gather(h_tile, 'col', axis=1, tiled=True)]
    all_gather x1 -> x0, waiting for transfers between devices: 40 us -> none  [shards(): lax.all_gather(p_tile, 'row', axis=0, tiled=True)]
    ppermute x0 -> x7, waiting for transfers between devices: none -> 22.7 us  [the longest x4 22.7 us: collect(): lower.append(lax.ppermute(lower[-1] if lower else value, axis, pairs))]
    ppermute x0 -> x7, starting transfers between devices: none -> 12 us  [the longest x3 10 us: collect(): upper.append(lax.ppermute(upper[-1] if upper else value, axis, back))]
    unnamed x10 -> x17, local copies, waits for them, and re-layouts: 0.03 us -> 5.09 us
    gather x0 -> x2, local copies, waits for them, and re-layouts: none -> 4.33 us  [collect(): tiles = tiles[(jnp.arange(length) - shift) % length]]
  transfers between devices with their start and end apart: 6 -> 12, of which waited for: 6 -> 9; matrix products, arithmetic and copies ran while one was open for 4% -> 7% of each run, Pallas kernels for 0% -> 0%
where the time goes in v1:
time: 363 us
  waiting for transfers between devices  269 us (74%)
  matrix products  44.6 us (12%)
  local copies, waits for them, and re-layouts  16.3 us (4%)
  between operations  16.1 us (4%)
  starting transfers between devices  12.4 us (3%)
  other arithmetic  4.08 us (1%)
    psum x1, waiting for transfers between devices, from_root(): return lax.psum(kept, axis)  83.7 us
    all_gather x1, waiting for transfers between devices, shards(): y_panel = lax.all_gather(y_tile, 'col', axis=1, tiled=True)  60.3 us
    all_gather x1, waiting for transfers between devices, shards(): lax.all_gather(s_tile, 'col', axis=1, tiled=True)  49.6 us
    all_gather x1, waiting for transfers between devices, shards(): lax.all_gather(s_tile, 'row', axis=0, tiled=True)  39.8 us
    ppermute x4, waiting for transfers between devices, collect(): lower.append(lax.ppermute(lower[-1] if lower else value, axis, pairs))  22.7 us
    dot_general x1, matrix products, shards(): jnp.dot(lax.all_gather(h_tile, 'col', axis=1, tiled=True), p_columns, pre...  16.6 us
    dot_general x1, matrix products, shards(): lax.dot_general(lax.all_gather(s_tile, 'col', axis=1, tiled=True), y_mirr...  16 us
    all_gather x1, waiting for transfers between devices, shards(): lax.all_gather(h_tile, 'col', axis=1, tiled=True)  12.5 us
  transfers between devices with their start and end apart: 12, of which 9 were waited for; matrix products, arithmetic and copies ran while one was open for 7% of the time, Pallas kernels for 0%

profile of v1, /device:TPU:2, one launch (start us, length us, event | category | flops | bytes accessed | tf_op | source)
XLA Modules:
  0.0 362.8 jit_solution(16053600532998431220)
XLA Ops:
  6.5 1.2 dot_general.31
  8.4 1.3 convolution_bitcast_fusion.2
  10.0 0.9 reshape.241
  13.0 2.0 collective-permute-start
  15.0 10.2 %collective-permute-done = f32[512,128]{0,1:T(8,128)S(1)} collective-permute-done((f32[512,128]{0,1:T(8,128)S(1)}, f32[512,128]{0,1:T(8,128)S(1)}, u32[]{:S(2)}, u32[]{:S(2)}) %collective-permute-start) | collective-permute-done | bytes 262176 | tf_op jit(solution)/shard_map/ppermute | solution.py:23
  25.2 3.2 collective-permute-start.4
  28.5 5.5 %collective-permute-done.1 = f32[512,128]{0,1:T(8,128)S(1)} collective-permute-done((f32[512,128]{0,1:T(8,128)S(1)}, f32[512,128]{0,1:T(8,128)S(1)}, u32[]{:S(2)}, u32[]{:S(2)}) %collective-permute-start.1) | collective-permute-done | bytes 262176 | tf_op jit(solution)/shard_map/ppermute | solution.py:23
  34.6 3.3 collective-permute-start.5
  37.9 3.8 %collective-permute-done.2 = f32[512,128]{0,1:T(8,128)S(1)} collective-permute-done((f32[512,128]{0,1:T(8,128)S(1)}, f32[512,128]{0,1:T(8,128)S(1)}, u32[]{:S(2)}, u32[]{:S(2)}) %collective-permute-start.2) | collective-permute-done | bytes 262176 | tf_op jit(solution)/shard_map/ppermute | solution.py:23
  42.6 3.5 collective-permute-start.6
  46.1 3.2 collective-permute-done.3
  55.1 2.4 gather_fusion
  57.6 1.9 copy.38
  59.4 12.5 %all-gather.5.cloned.1.call-done = f32[512,4096]{0,1:T(8,128)} async-done(((f32[512,128]{0,1:T(8,128)}), f32[512,4096]{0,1:T(8,128)}) %all-gather.5.cloned.1.call-update) | async-done | bytes 8388624 | tf_op jit(solution)/shard_map/all_gather | solution.py:100
  71.9 16.6 %convolution_multiply_fusion = f32[512,128]{1,0:T(8,128)} fusion(f32[512,128]{1,0:T(8,128)S(1)} %reshape.240, f32[512,4096]{0,1:T(8,128)} %all-gather.5.cloned.1.call-done, f32[4096,128]{1,0:T(8,128)} %bitcast.108), kind=kOutput, calls=%fused_computation.8 | convolution fusion | flops 3221291008 | bytes 11010048 | tf_op jit(solution)/shard_map/dot_general | solution.py:99
  90.4 0.9 reshape.244
  92.2 60.3 %all-gather.7.cloned.1.call-done = f32[512,4096]{1,0:T(8,128)} async-done(((f32[512,128]{1,0:T(8,128)}), f32[512,4096]{1,0:T(8,128)}) %all-gather.7.cloned.1.call-update) | async-done | bytes 8388624 | tf_op jit(solution)/shard_map/all_gather | solution.py:105
  152.6 3.1 dynamic-slice_select_fusion
  155.8 39.8 %all-gather.9.cloned.1.call-done = f32[4096,128]{0,1:T(8,128)} async-done(((f32[512,128]{0,1:T(8,128)}), f32[4096,128]{0,1:T(8,128)}) %all-gather.9.cloned.1.call-update) | async-done | bytes 2097168 | tf_op jit(solution)/shard_map/all_gather | solution.py:97
  195.6 9.3 %fusion.31 = f32[512,128]{1,0:T(8,128)S(1)} fusion(f32[512,4096]{1,0:T(8,128)} %all-gather.7.cloned.1.call-done, f32[4096,128]{0,1:T(8,128)} %all-gather.9.cloned.1.call-done), kind=kOutput, calls=%fused_computation.64 | convolution fusion | flops 3221225472 | bytes 10747904 | tf_op jit(solution)/shard_map/dot_general | solution.py:106
  205.0 49.6 %all-gather.11.cloned.1.call-done = f32[512,4096]{0,1:T(8,128)} async-done(((f32[512,128]{0,1:T(8,128)}), f32[512,4096]{0,1:T(8,128)}) %all-gather.11.cloned.1.call-update) | async-done | bytes 8388624 | tf_op jit(solution)/shard_map/all_gather | solution.py:113
  254.5 83.7 %all-reduce.2.cloned.1.call-done = f32[128,4096]{1,0:T(8,128)} async-done(((f32[128,4096]{1,0:T(8,128)}), f32[128,4096]{1,0:T(8,128)}) %all-reduce.2.cloned.1.call-update) | async-done | bytes 2097168 | tf_op jit(solution)/shard_map/psum | solution.py:34
  338.3 16.0 %fusion = f32[512,128]{1,0:T(8,128)S(1)} fusion(f32[512,128]{1,0:T(8,128)S(1)} %reshape.240, f32[512,128]{1,0:T(8,128)S(1)} %fusion.31, f32[512,4096]{0,1:T(8,128)} %all-gather.11.cloned.1.call-done, f32[128,4096]{1,0:T(8,128)} %all-reduce.2.cloned.1.call-done), kind=kOutput, calls=%fused_computation.7 | convolution fusion | flops 3221356544 | bytes 11272192 | tf_op jit(solution)/shard_map/dot_general | solution.py:112
  355.5 0.8 fusion.7
  (61 shorter events, 11.6 us)
Async XLA Ops:
  6.5 4.4 %copy-start = (f32[1,16,4096]{2,1,0:T(8,128)S(1)}, f32[1,16,4096]{2,1,0:T(8,128)}, u32[]{:S(2)}) copy-start(f32[1,16,4096]{2,1,0:T(8,128)} %param.14) | copy-start | bytes 786436
  6.5 65.4 %all-gather.5.cloned.1.call-start = ((), (), s32[]{:S(2)}) async-start(), calls=%async_computation | async-start | bytes 8650752 | tf_op jit(solution)/shard_map/all_gather | solution.py:100
  7.7 4.1 %copy-start.2 = (s32[1,16]{1,0:T(1,128)S(1)}, s32[1,16]{1,0:T(1,128)}, u32[]{:S(2)}) copy-start(s32[1,16]{1,0:T(1,128)} %param.15) | copy-start | bytes 196
  10.9 30.8 %copy-start.4 = (s32[1,16]{1,0:T(1,128)S(1)}, s32[1,16]{1,0:T(1,128)}, u32[]{:S(2)}) copy-start(s32[1,16]{1,0:T(1,128)} %param.20) | copy-start | bytes 196
  10.9 141.7 %all-gather.7.cloned.1.call-start = ((), (), s32[]{:S(2)}) async-start(), calls=%async_computation.1 | async-start | bytes 8650752 | tf_op jit(solution)/shard_map/all_gather | solution.py:105
  13.0 12.2 %collective-permute-start = (f32[512,128]{0,1:T(8,128)S(1)}, f32[512,128]{0,1:T(8,128)S(1)}, u32[]{:S(2)}, u32[]{:S(2)}) collective-permute-start(f32[512,128]{0,1:T(8,128)S(1)} %reshape.242), channel_id=1, source_target_pairs={{0,32},{32,64},{64,96},{96,128},{128,160},{160,192},{192,224},{224... | collective-permute-start | bytes 786440 | tf_op jit(solution)/shard_map/ppermute | solution.py:23
  25.2 8.7 %collective-permute-start.1 = (f32[512,128]{0,1:T(8,128)S(1)}, f32[512,128]{0,1:T(8,128)S(1)}, u32[]{:S(2)}, u32[]{:S(2)}) collective-permute-start(f32[512,128]{0,1:T(8,128)S(1)} %collective-permute-done), channel_id=1, source_target_pairs={{0,32},{32,64},{64,96},{96,128},{128,160},{160,192},{192,224},{224... | collective-permute-start | bytes 786440 | tf_op jit(solution)/shard_map/ppermute | solution.py:23
  25.2 9.4 %collective-permute-start.4 = (f32[512,128]{0,1:T(8,128)S(1)}, f32[512,128]{0,1:T(8,128)S(1)}, u32[]{:S(2)}, u32[]{:S(2)}) collective-permute-start(f32[512,128]{0,1:T(8,128)S(1)} %reshape.242), channel_id=1, source_target_pairs={{32,0},{64,32},{96,64},{128,96},{160,128},{192,160},{224,192},{0,2... | collective-permute-start | bytes 786440 | tf_op jit(solution)/shard_map/ppermute | solution.py:25
  33.9 7.8 %collective-permute-start.2 = (f32[512,128]{0,1:T(8,128)S(1)}, f32[512,128]{0,1:T(8,128)S(1)}, u32[]{:S(2)}, u32[]{:S(2)}) collective-permute-start(f32[512,128]{0,1:T(8,128)S(1)} %collective-permute-done.1), channel_id=1, source_target_pairs={{0,32},{32,64},{64,96},{96,128},{128,160},{160,192},{192,224},{224... | collective-permute-start | bytes 786440 | tf_op jit(solution)/shard_map/ppermute | solution.py:23
  34.6 8.0 %collective-permute-start.5 = (f32[512,128]{0,1:T(8,128)S(1)}, f32[512,128]{0,1:T(8,128)S(1)}, u32[]{:S(2)}, u32[]{:S(2)}) collective-permute-start(f32[512,128]{0,1:T(8,128)S(1)} %collective-permute-done.4), channel_id=1, source_target_pairs={{32,0},{64,32},{96,64},{128,96},{160,128},{192,160},{224,192},{0,2... | collective-permute-start | bytes 786440 | tf_op jit(solution)/shard_map/ppermute | solution.py:25
  41.7 7.6 %collective-permute-start.3 = (f32[512,128]{0,1:T(8,128)S(1)}, f32[512,128]{0,1:T(8,128)S(1)}, u32[]{:S(2)}, u32[]{:S(2)}) collective-permute-start(f32[512,128]{0,1:T(8,128)S(1)} %collective-permute-done.2), channel_id=1, source_target_pairs={{0,32},{32,64},{64,96},{96,128},{128,160},{160,192},{192,224},{224... | collective-permute-start | bytes 786440 | tf_op jit(solution)/shard_map/ppermute | solution.py:23
  42.6 11.8 %collective-permute-start.6 = (f32[512,128]{0,1:T(8,128)S(1)}, f32[512,128]{0,1:T(8,128)S(1)}, u32[]{:S(2)}, u32[]{:S(2)}) collective-permute-start(f32[512,128]{0,1:T(8,128)S(1)} %collective-permute-done.5), channel_id=1, source_target_pairs={{32,0},{64,32},{96,64},{128,96},{160,128},{192,160},{224,192},{0,2... | collective-permute-start | bytes 786440 | tf_op jit(solution)/shard_map/ppermute | solution.py:25
  71.9 16.7 %copy-start.1 = (f32[1,16,4096]{2,1,0:T(8,128)S(1)}, f32[1,16,4096]{2,1,0:T(8,128)}, u32[]{:S(2)}) copy-start(f32[1,16,4096]{2,1,0:T(8,128)} %param.17) | copy-start | bytes 786436
  71.9 17.5 %copy-start.3 = (s32[1,16]{1,0:T(1,128)S(1)}, s32[1,16]{1,0:T(1,128)}, u32[]{:S(2)}) copy-start(s32[1,16]{1,0:T(1,128)} %param.18) | copy-start | bytes 196
  88.5 107.1 %all-gather.9.cloned.1.call-start = ((), (), s32[]{:S(2)}) async-start(), calls=%async_computation.2 | async-start | bytes 2359296 | tf_op jit(solution)/shard_map/all_gather | solution.py:97
  91.4 163.2 %all-gather.11.cloned.1.call-start = ((), (), s32[]{:S(2)}) async-start(), calls=%async_computation.3 | async-start | bytes 8650752 | tf_op jit(solution)/shard_map/all_gather | solution.py:113
  91.9 246.3 %all-reduce.2.cloned.1.call-start = ((), (), s32[]{:S(2)}) async-start(), calls=%async_computation.4 | async-start | bytes 4194304 | tf_op jit(solution)/shard_map/psum | solution.py:34
Sparse Core Ops, SparseCore 0:
  11.0 60.8 all-gather.4
  88.6 63.8 all-gather.6
  154.4 41.1 all-gather.8
  198.0 56.4 all-gather.10
  256.7 81.4 all-reduce.1
